TPU v7x, 32 devices: a whole 2x2x4 slice. The times are simulated.
32 devices in a mesh: rep: 16 (over z, x, core), fsdp: 2 (over y).
Axes of the slice: x: 2, y: 2, z: 4, core: 2. Of those that a mesh axis runs over, the one named last changes fastest.
Arguments:
- contexts: bfloat16 [16, 256, 2048], P('rep', 'fsdp'), may hold values from -6 to 6
- residual: bfloat16 [16, 256, 4096], P('rep', 'fsdp'), may hold values from -6 to 6
- cotangent: bfloat16 [16, 256, 4096], P('rep', 'fsdp'), may hold values from -96 to 96
- token_ids: int32 [16, 256], P('rep', 'fsdp'), may hold values from 0 to 31999, as said below
- step_index: int32 [1], replicated, may hold values from 0 to 999
- weight: bfloat16 [16, 2048, 4096], P('rep', None, 'fsdp'), may hold values from -0.125 to 0.125
- norm_gain: bfloat16 [16, 4096], P('rep', 'fsdp'), may hold values from 0.5 to 1.5
- momentum: bfloat16 [16, 2048, 4096], P('rep', None, 'fsdp'), may hold values from -6 to 6
- gain_momentum: bfloat16 [16, 4096], P('rep', 'fsdp'), may hold values from -6 to 6
Outputs:
- new_weight: bfloat16 [16, 2048, 4096], P('rep', None, 'fsdp')
- new_gain: bfloat16 [16, 4096], P('rep', 'fsdp')
- new_momentum: bfloat16 [16, 2048, 4096], P('rep', None, 'fsdp')
- new_gain_momentum: bfloat16 [16, 4096], P('rep', 'fsdp')
Inputs may be any that keep to these rules, and one draw needn't show every extreme that they name: `token_ids`: ids of 31744 and above are action tokens; the last token of every replica is one.
All inputs are finite; a program needn't handle non-finite values.
Results may differ from a plain program's by a relative error of at most 0.0095.
Values may be sent and summed in bfloat16 or wider, within the bound.
No kernel may reach another device: no remote copies, remote signals or barrier semaphores. Data moves between devices by JAX's collectives and lax.ppermute only.
A program may use at most 128 MiB of HBM per device.

v0:
```python
import functools
import math

import jax
import jax.numpy as jnp
from jax import lax
from jax.experimental import pallas as pl
from jax.experimental.pallas import tpu as pltpu
from jax.sharding import PartitionSpec as P

VOCAB = 32000
ACTION = 256


EPSILON = 1e-05
BETA = 0.9
LEARN_RATE = 0.05


SHARES = (48, 12, 3, 1)
NEAR = 2
LANES = 128
TILE = 16


def passed_along(array, axis, by):
    peers = lax.axis_size(axis)
    return lax.ppermute(array, axis, [(i, (i + by) % peers) for i in range(peers)])


def cost(flops, *arrays):
    moved = sum(array.size * array.dtype.itemsize for array in arrays)
    return pl.CostEstimate(flops=flops, bytes_accessed=moved, transcendentals=0)


def vmem(*blocks):
    room = sum(2 * size * math.prod(shape) for shape, size in blocks) + 3 * 2**20
    return pltpu.CompilerParams(vmem_limit_bytes=room)


def largest_block(size, most):
    return max(block for block in range(1, most + 1) if size % block == 0)


def forward_kernel(count_ref, ctx_ref, weight_ref, resid_ref, cotan_ref, gain_ref, pre_ref, sums_ref):
    tokens, _ = resid_ref.shape
    strip = largest_block(tokens, 128)
    at = pl.program_id(0)
    lane = lax.broadcasted_iota(jnp.int32, (strip, LANES), 1)

    @pl.when(at == 0)
    def _():
        sums_ref[...] = jnp.where(
            lax.broadcasted_iota(jnp.int32, sums_ref.shape, 1) == 2, count_ref[0], 0.0
        )

    def one_strip(i, carry):
        rows = pl.ds(pl.multiple_of(i * strip, strip), strip)
        pre = resid_ref[rows, :].astype(jnp.float32) + jnp.dot(
            ctx_ref[rows, :], weight_ref[...], preferred_element_type=jnp.float32
        )
        pre_ref[rows, :] = pre
        weighted = cotan_ref[rows, :].astype(jnp.float32) * gain_ref[...].astype(jnp.float32)
        square = jnp.sum(pre * pre, axis=1, keepdims=True)
        inner = jnp.sum(weighted * pre, axis=1, keepdims=True)
        sums_ref[rows, :] += jnp.where(lane == 0, square, jnp.where(lane == 1, inner, 0.0))
        return carry

    lax.fori_loop(0, tokens // strip, one_strip, 0)


def forward(own_count, ctx, weight, resid, cotan, gain):
    tokens, columns = resid.shape
    hidden = ctx.shape[1]
    block = largest_block(columns, 256)
    out = [
        jax.ShapeDtypeStruct((tokens, columns), jnp.float32),
        jax.ShapeDtypeStruct((tokens, LANES), jnp.float32),
    ]
    by_columns = pl.BlockSpec((tokens, block), lambda i: (0, i))
    return pl.pallas_call(
        forward_kernel,
        grid=(columns // block,),
        in_specs=[
            pl.BlockSpec(memory_space=pltpu.SMEM),
            pl.BlockSpec((tokens, hidden), lambda i: (0, 0)),
            pl.BlockSpec((None, hidden, block), lambda i: (0, 0, i)),
            by_columns,
            by_columns,
            pl.BlockSpec((1, block), lambda i: (0, i)),
        ],
        out_specs=[by_columns, pl.BlockSpec((tokens, LANES), lambda i: (0, 0))],
        out_shape=out,
        compiler_params=vmem(
            ((tokens, hidden), 2), ((hidden, block), 2), ((tokens, block), 8), ((tokens, LANES), 4)
        ),
        cost_estimate=cost(2 * tokens * hidden * columns, ctx, weight, resid, cotan, *out),
        name="forward",
    )(own_count, ctx, weight, resid, cotan, gain)


def gradient_kernel(
    width, pre_ref, cotan_ref, sums_ref, gain_ref, gain_momentum_ref, grad_ref, gains_ref
):
    tokens, columns = pre_ref.shape
    gain = gain_ref[...].astype(jnp.float32)

    def one_strip(i, grad_gain):
        rows = pl.ds(pl.multiple_of(i * TILE, TILE), TILE)
        inverse = lax.rsqrt(sums_ref[rows, 0:1] / width + EPSILON)
        share = 1.0 / sums_ref[rows, 2:3]
        inner = inverse * (sums_ref[rows, 1:2] * share) / width
        normed = pre_ref[rows, :] * inverse
        scaled = cotan_ref[rows, :].astype(jnp.float32) * share
        grad = inverse * (scaled * gain - normed * inner)
        grad_ref[rows, :] = grad.astype(jnp.bfloat16)
        product = scaled * normed
        return grad_gain + (product[: TILE // 2] + product[TILE // 2 :])

    grad_gain = lax.fori_loop(
        0, tokens // TILE, one_strip, jnp.zeros((TILE // 2, columns), jnp.float32)
    )
    grad_gain = jnp.sum(grad_gain, axis=0, keepdims=True)
    mom = (BETA * gain_momentum_ref[...].astype(jnp.float32) + grad_gain).astype(jnp.bfloat16)
    mom = mom.astype(jnp.float32)
    par = (gain - LEARN_RATE * mom).astype(jnp.bfloat16).astype(jnp.float32)
    row = lax.broadcasted_iota(jnp.int32, gains_ref.shape, 0)
    gains_ref[...] = jnp.where(row == 0, par, mom).astype(jnp.bfloat16)


def gradient(width, pre, cotan, sums, gain, gain_momentum):
    tokens, columns = pre.shape
    block = largest_block(columns, 1024)
    out = [
        jax.ShapeDtypeStruct((tokens, columns), jnp.bfloat16),
        jax.ShapeDtypeStruct((2, columns), jnp.bfloat16),
    ]
    by_columns = pl.BlockSpec((tokens, block), lambda i: (0, i))
    one_row = pl.BlockSpec((1, block), lambda i: (0, i))
    return pl.pallas_call(
        functools.partial(gradient_kernel, width),
        grid=(columns // block,),
        in_specs=[
            by_columns,
            by_columns,
            pl.BlockSpec((tokens, LANES), lambda i: (0, 0)),
            one_row,
            one_row,
        ],
        out_specs=[by_columns, pl.BlockSpec((2, block), lambda i: (0, i))],
        out_shape=out,
        compiler_params=vmem(((tokens, block), 8), ((tokens, LANES), 4), ((8, block), 6)),
        cost_estimate=cost(12 * tokens * columns, pre, cotan, sums, *out),
        name="gradient",
    )(pre, cotan, sums, gain, gain_momentum)


def momentum_rows_kernel(ctx_ref, grad_ref, momentum_ref, out_ref):
    columns = momentum_ref.shape[1]
    part = largest_block(columns, 512)

    def one_part(i, carry):
        at = pl.ds(pl.multiple_of(i * part, part), part)
        grad_weight = jnp.dot(ctx_ref[...], grad_ref[:, at], preferred_element_type=jnp.float32)
        mom = BETA * momentum_ref[:, at].astype(jnp.float32) + grad_weight
        out_ref[:, at] = mom.astype(jnp.bfloat16)
        return carry

    lax.fori_loop(0, columns // part, one_part, 0)


def momentum_rows(ctx_t, grad_pre, momentum, first, rows, block):
    tokens, columns = grad_pre.shape
    skip = first // block
    return pl.pallas_call(
        momentum_rows_kernel,
        grid=(rows // block,),
        in_specs=[
            pl.BlockSpec((block, tokens), lambda i: (skip + i, 0)),
            pl.BlockSpec((tokens, columns), lambda i: (0, 0)),
            pl.BlockSpec((None, block, columns), lambda i: (0, skip + i, 0)),
        ],
        out_specs=pl.BlockSpec((block, columns), lambda i: (i, 0)),
        out_shape=jax.ShapeDtypeStruct((rows, columns), jnp.bfloat16),
        compiler_params=vmem(((block, tokens), 2), ((tokens, columns), 2), ((block, columns), 4)),
        cost_estimate=pl.CostEstimate(
            flops=2 * rows * tokens * columns,
            bytes_accessed=4 * rows * columns + 2 * tokens * (rows + columns),
            transcendentals=0,
        ),
        name="momentum_rows",
    )(ctx_t, grad_pre, momentum)


def new_parameter(old, mom):
    return (old.astype(jnp.float32) - LEARN_RATE * mom.astype(jnp.float32)).astype(jnp.bfloat16)


def average_block(
    weight_ref, far_weight_ref, mom_ref, far_mom_ref, out_weight_ref, out_mom_ref, weight_first=0
):
    rows, columns = out_weight_ref.shape
    part = largest_block(columns, 2048)
    parts = columns // part
    half = jnp.bfloat16(0.5)
    first = pl.program_id(0) * rows

    def one_part(i, carry):
        row = i // parts * TILE
        column = pl.ds(pl.multiple_of(i % parts * part, part), part)
        out = (pl.ds(pl.multiple_of(row, TILE), TILE), column)
        at = (pl.ds(pl.multiple_of(first + row, TILE), TILE), column)
        mom, far_mom = mom_ref[at], far_mom_ref[at]
        old = (pl.ds(pl.multiple_of(weight_first + row, TILE), TILE), column)
        par = new_parameter(weight_ref[old], mom) + new_parameter(far_weight_ref[old], far_mom)
        out_weight_ref[out] = par * half
        out_mom_ref[out] = (mom + far_mom) * half
        return carry

    lax.fori_loop(0, rows // TILE * parts, one_part, 0)


def average_rows_kernel(weight_ref, far_weight_ref, mom_ref, far_mom_ref, *refs):
    average_block(weight_ref, far_weight_ref, mom_ref, far_mom_ref, *refs[-2:])


def average_cost(rows, columns):
    return pl.CostEstimate(
        flops=8 * rows * columns, bytes_accessed=12 * rows * columns, transcendentals=0
    )


def average_rows(weight, far_weight, mom, far_mom, held, first, block, ready):
    rows, columns = mom.shape
    skip = first // block
    whole = pl.BlockSpec((None, block, columns), lambda i: (0, skip + i, 0))
    chunk = pl.BlockSpec(memory_space=pltpu.VMEM)
    shape = pltpu.HBM(weight.shape, jnp.bfloat16)
    return pl.pallas_call(
        average_rows_kernel,
        grid=(rows // block,),
        in_specs=[whole, whole, chunk, chunk] + [pl.BlockSpec(memory_space=pl.ANY)] * (len(held) + 1),
        out_specs=[whole, whole],
        out_shape=[shape, shape],
        input_output_aliases={4 + at: at for at in range(len(held))},
        compiler_params=vmem(((block, columns), 12)),
        cost_estimate=average_cost(rows, columns),
        name="average_rows",
    )(weight, far_weight, mom, far_mom, *held, ready)


def average_near_kernel(weight_first, *refs):
    outs = refs[8 if len(refs) == 12 else 6 :]
    first = weight_first + pl.program_id(0) * outs[0].shape[0]
    average_block(*refs[:4], *outs[:2], first)
    if len(outs) == 2:
        return
    gains_ref, far_gains_ref = refs[4:6]

    @pl.when(pl.program_id(0) == 0)
    def _():
        gains = gains_ref[...].astype(jnp.float32) + far_gains_ref[...].astype(jnp.float32)
        gains = (gains * 0.5).astype(jnp.bfloat16)
        outs[2][...] = gains[0:1]
        outs[3][...] = gains[1:2]


def average_near(weight, far_weight, mom, far_mom, held, first, weight_first, gains):
    rows, columns = mom.shape
    block = math.gcd(first, rows, 32)
    skip = first // block
    inputs = (weight, far_weight, mom, far_mom, *gains)
    whole = pl.BlockSpec((None, block, columns), lambda i: (0, skip + i, 0))
    shape = pltpu.HBM(held[0].shape, jnp.bfloat16)
    one_row = pl.BlockSpec((1, columns), lambda i: (0, 0))
    row_shape = jax.ShapeDtypeStruct((1, columns), jnp.bfloat16)
    return pl.pallas_call(
        functools.partial(average_near_kernel, weight_first),
        grid=(rows // block,),
        in_specs=[pl.BlockSpec(memory_space=pltpu.VMEM)] * len(inputs)
        + [pl.BlockSpec(memory_space=pl.ANY)] * 2,
        out_specs=[whole, whole] + [one_row for _ in gains],
        out_shape=[shape, shape] + [row_shape for _ in gains],
        input_output_aliases={len(inputs): 0, len(inputs) + 1: 1},
        compiler_params=vmem((weight.shape, 4), ((rows, columns), 4), ((block, columns), 4)),
        cost_estimate=average_cost(rows, columns),
        name="average_near",
    )(*inputs, *held)


def replica_step(
    contexts,
    residual,
    cotangent,
    token_ids,
    weight,
    norm_gain,
    momentum,
    gain_momentum,
    *,
    level,
):
    distance = 1 << level
    me, peers = lax.axis_index("fsdp"), lax.axis_size("fsdp")
    tokens = contexts.shape[1]
    hidden, columns = weight.shape[1:]

    far_weight = passed_along(weight, "rep", distance)

    def from_all(block_for):
        parts = [block_for(me)]
        for shift in range(1, peers):
            parts.append(passed_along(block_for((me + shift) % peers), "fsdp", shift))
        return jnp.concatenate(parts)

    def columns_of(array):
        return lambda peer: lax.dynamic_slice_in_dim(array, peer * columns, columns, 1)

    action = token_ids[0] >= VOCAB - ACTION
    own_count = jnp.sum(action.astype(jnp.float32)).reshape(1)
    masked = jnp.where(action[:, None], cotangent[0], jnp.zeros((), cotangent.dtype))
    ctx = from_all(lambda peer: contexts[0])
    resid = from_all(columns_of(residual[0]))
    cotan = from_all(columns_of(masked))

    pre, sums = forward(own_count, ctx, weight, resid, cotan, norm_gain)
    total = sums
    for shift in range(1, peers):
        total = total + jnp.roll(passed_along(sums, "fsdp", shift), shift * tokens, 0)
    grad_pre, gains = gradient(columns * peers, pre, cotan, total, norm_gain, gain_momentum)
    far_gains = passed_along(gains, "rep", distance)

    unit = hidden // sum(SHARES)
    ctx_t = ctx.T
    first, held = 0, ()
    near = hidden - sum(SHARES[-NEAR:]) * unit
    near_weight, far_near_weight = weight[0, near:], far_weight[0, near:]
    for share in SHARES:
        rows = share * unit
        block = math.gcd(first, rows, 128)
        mom = momentum_rows(ctx_t, grad_pre, momentum, first, rows, block)
        far_mom = passed_along(mom, "rep", distance)
        if first < near:
            held = average_rows(weight, far_weight, mom, far_mom, held, first, block, far_near_weight)
        else:
            sent = (gains, far_gains) if first + rows == hidden else ()
            held = average_near(
                near_weight, far_near_weight, mom, far_mom, held, first, first - near, sent
            )
        first += rows
    new_weight, new_momentum, new_gain, new_gain_momentum = held
    return new_weight, new_gain, new_momentum, new_gain_momentum


def shards(
    contexts, residual, cotangent, token_ids, step_index, weight, norm_gain, momentum, gain_momentum
):
    levels = lax.axis_size("rep").bit_length() - 1

    def branch(level):
        def run(*arrays):
            return replica_step(*arrays, level=level)

        return run

    branches = [branch(level) for level in range(levels)]
    return lax.switch(
        lax.rem(step_index[0], levels),
        branches,
        contexts,
        residual,
        cotangent,
        token_ids,
        weight,
        norm_gain,
        momentum,
        gain_momentum,
    )


def solution(mesh):
    placed = (
        P("rep", "fsdp", None),
        P("rep", "fsdp", None),
        P("rep", "fsdp", None),
        P("rep", "fsdp"),
        P(),
        P("rep", None, "fsdp"),
        P("rep", "fsdp"),
        P("rep", None, "fsdp"),
        P("rep", "fsdp"),
    )
    return jax.shard_map(
        shards,
        mesh=mesh,
        in_specs=placed,
        out_specs=(
            P("rep", None, "fsdp"),
            P("rep", "fsdp"),
            P("rep", None, "fsdp"),
            P("rep", "fsdp"),
        ),
        check_vma=False,
    )
```

profile of v0, /device:TPU:0, one launch (start us, length us, event | category | flops | bytes accessed | tf_op | source)
XLA Modules:
  0.0 193.9 jit_solution(12478516044785466451)
XLA Ops:
  1.3 192.6 %conditional.1 = (bf16[1,2048,2048]{2,1,0:T(8,128)(2,1)}, bf16[1,2048]{1,0:T(2,128)(2,1)}, bf16[1,2048,2048]{2,1,0:T(8,128)(2,1)}, bf16[1,2048]{1,0:T(2,128)(2,1)}) conditional(s32[]{:T(128)} %clamp.3, (bf16[1,2048,2048]{2,1,0:T(8,128)(2,1)}, bf16[1,128,2048]{2,1,0:T(8,128)(2,1)}, s32[1,128]{1,0:T(1,128)}, ...), branch_computations={%region_0.2_spmd, %region_2.4_spmd, %region_4.6_spmd, %region_6.8_... | conditional | flops 4341694976 | bytes 234303584 | solution.py:367
  2.6 3.1 %collective-permute-start.1 = (bf16[128,2048]{0,1:T(8,128)(2,1)S(1)}, bf16[128,2048]{0,1:T(8,128)(2,1)S(1)}, u32[]{:S(2)}, u32[]{:S(2)}) collective-permute-start(bf16[128,2048]{0,1:T(8,128)(2,1)S(1)} %bitcast.92), channel_id=1, source_target_pairs={{0,1},{1,0},{2,3},{3,2},{4,5},{5,4},{6,7},{7,6},{8,9},{9,8},{10,11... | collective-permute-start | bytes 1572872 | tf_op jit(solution)/shard_map/cond/branch_0_fun/ppermute | solution.py:28
  6.4 1.4 bitcast_select_fusion
  8.9 2.3 %dynamic-slice_bitcast_fusion.1 = (bf16[128,2048]{1,0:T(8,128)(2,1)}, bf16[128,2048]{1,0:T(8,128)(2,1)}) fusion(bf16[1,128,4096]{2,1,0:T(8,128)(2,1)} %get-tuple-element.67, s32[]{:T(128)S(6)} %select_n.56, s32[]{:T(128)S(6)} %select_n.58), kind=kLoop, calls=%fused_computation.6 | loop fusion | bytes 2097160 | tf_op jit(solution)/shard_map/cond/branch_0_fun/dynamic_slice | solution.py:317
  11.2 1.9 %collective-permute-start.2 = (bf16[128,2048]{1,0:T(8,128)(2,1)}, bf16[128,2048]{1,0:T(8,128)(2,1)}, u32[]{:S(2)}, u32[]{:S(2)}) collective-permute-start(bf16[128,2048]{1,0:T(8,128)(2,1)} %get-tuple-element.191), channel_id=1, source_target_pairs={{0,1},{1,0},{2,3},{3,2},{4,5},{5,4},{6,7},{7,6},{8,9},{9,8},{10,11... | collective-permute-start | bytes 1572872 | tf_op jit(solution)/shard_map/cond/branch_0_fun/ppermute | solution.py:28
  13.7 4.8 %collective-permute-done.1 = bf16[128,2048]{0,1:T(8,128)(2,1)S(1)} collective-permute-done((bf16[128,2048]{0,1:T(8,128)(2,1)S(1)}, bf16[128,2048]{0,1:T(8,128)(2,1)S(1)}, u32[]{:S(2)}, u32[]{:S(2)}) %collective-permute-start.1) | collective-permute-done | bytes 524320 | tf_op jit(solution)/shard_map/cond/branch_0_fun/ppermute | solution.py:28
  19.3 10.5 %collective-permute-done.3 = bf16[128,2048]{1,0:T(8,128)(2,1)} collective-permute-done((bf16[128,2048]{1,0:T(8,128)(2,1)}, bf16[128,2048]{1,0:T(8,128)(2,1)}, u32[]{:S(2)}, u32[]{:S(2)}) %collective-permute-start.3) | collective-permute-done | bytes 524320 | tf_op jit(solution)/shard_map/cond/branch_0_fun/ppermute | solution.py:28
  31.1 9.1 %collective-permute-done.2 = bf16[128,2048]{1,0:T(8,128)(2,1)} collective-permute-done((bf16[128,2048]{1,0:T(8,128)(2,1)}, bf16[128,2048]{1,0:T(8,128)(2,1)}, u32[]{:S(2)}, u32[]{:S(2)}) %collective-permute-start.2) | collective-permute-done | bytes 524320 | tf_op jit(solution)/shard_map/cond/branch_0_fun/ppermute | solution.py:28
  41.5 10.5 %forward.4 = (f32[256,2048]{1,0:T(8,128)S(1)}, f32[256,128]{1,0:T(8,128)S(1)}) custom-call(f32[1]{0:T(128)} %bitcast.5.count_ref, bf16[256,2048]{1,0:T(8,128)(2,1)S(1)} %copy.37.ctx_ref, bf16[1,2048,2048]{2,1,0:T(8,128)(2,1)} %get-tuple-element.64.weight_ref, bf16[256,2048]{1,0:T(8,128)(2,1)S(1)} %pad_maximum_fusion.1.resid_ref, ...), custom_call_target="tpu_custom_call" | custom-call | flops 2147483648 | bytes 13762560 | tf_op jit(solution)/shard_map/cond/branch_0_fun/forward/pallas_call | solution.py:81
  52.1 1.8 collective-permute-start.4
  53.9 3.2 %collective-permute-done.4 = f32[256,128]{1,0:T(8,128)S(1)} collective-permute-done((f32[256,128]{1,0:T(8,128)S(1)}, f32[256,128]{1,0:T(8,128)S(1)}, u32[]{:S(2)}, u32[]{:S(2)}) %collective-permute-start.4) | collective-permute-done | bytes 131104 | tf_op jit(solution)/shard_map/cond/branch_0_fun/ppermute | solution.py:28
  57.1 7.5 %gradient.4 = (bf16[256,2048]{1,0:T(8,128)(2,1)S(1)}, bf16[2,2048]{1,0:T(2,128)(2,1)S(1)}) custom-call(f32[256,2048]{1,0:T(8,128)S(1)} %get-tuple-element.70.pre_ref, bf16[256,2048]{1,0:T(8,128)(2,1)S(1)} %pad_maximum_fusion.2.cotan_ref, f32[256,128]{1,0:T(8,128)S(1)} %maximum_add_fusion.sums_ref, bf16[1,2048]{1,0:T(2,128)(2,1)S(1)} %copy-done, ...), custom_call_target="tpu_custom_call" | custom-call | flops 6291456 | bytes 4333568 | tf_op jit(solution)/shard_map/cond/branch_0_fun/gradient/pallas_call | solution.py:140
  64.7 9.5 %momentum_rows.19.mom_ref = bf16[1536,2048]{1,0:T(8,128)(2,1)S(1)} custom-call(bf16[2048,256]{1,0:T(8,128)(2,1)S(1)} %get-tuple-element.193.ctx_ref, bf16[256,2048]{1,0:T(8,128)(2,1)S(1)} %get-tuple-element.73.grad_ref, bf16[1,2048,2048]{2,1,0:T(8,128)(2,1)S(1)} %bitcast.77), custom_call_target="tpu_custom_call" | custom-call | flops 1610612736 | bytes 14417920 | tf_op jit(solution)/shard_map/cond/branch_0_fun/momentum_rows/pallas_call | solution.py:175
  74.3 2.4 %momentum_rows.18.mom_ref = bf16[384,2048]{1,0:T(8,128)(2,1)S(1)} custom-call(bf16[2048,256]{1,0:T(8,128)(2,1)S(1)} %get-tuple-element.193.ctx_ref, bf16[256,2048]{1,0:T(8,128)(2,1)S(1)} %get-tuple-element.73.grad_ref, bf16[1,2048,2048]{2,1,0:T(8,128)(2,1)S(1)} %bitcast.77), custom_call_target="tpu_custom_call" | custom-call | flops 402653184 | bytes 4390912 | tf_op jit(solution)/shard_map/cond/branch_0_fun/momentum_rows/pallas_call | solution.py:175
  76.7 1.9 collective-permute-start.8
  79.3 1.6 collective-permute-start.5
  81.0 1.9 momentum_rows.17.refs_2_
  82.9 18.7 %collective-permute-done.far_weight_ref = bf16[1,2048,2048]{2,1,0:T(8,128)(2,1)} collective-permute-done((bf16[1,2048,2048]{2,1,0:T(8,128)(2,1)}, bf16[1,2048,2048]{2,1,0:T(8,128)(2,1)}, u32[]{:S(2)}, u32[]{:S(2)}) %collective-permute-start) | collective-permute-done | bytes 8388640 | tf_op jit(solution)/shard_map/cond/branch_0_fun/ppermute | solution.py:28
  102.7 66.2 %collective-permute-done.9.far_mom_ref = bf16[1536,2048]{1,0:T(8,128)(2,1)S(1)} collective-permute-done((bf16[1536,2048]{1,0:T(8,128)(2,1)S(1)}, bf16[1536,2048]{1,0:T(8,128)(2,1)S(1)}, u32[]{:S(2)}, u32[]{:S(2)}) %collective-permute-start.9) | collective-permute-done | bytes 6291488 | tf_op jit(solution)/shard_map/cond/branch_0_fun/ppermute | solution.py:28
  168.9 12.5 %average_rows.8 = (bf16[1,2048,2048]{2,1,0:T(8,128)(2,1)}, bf16[1,2048,2048]{2,1,0:T(8,128)(2,1)}) custom-call(bf16[1,2048,2048]{2,1,0:T(8,128)(2,1)S(1)} %bitcast.85, bf16[1,2048,2048]{2,1,0:T(8,128)(2,1)} %collective-permute-done.far_weight_ref, bf16[1536,2048]{1,0:T(8,128)(2,1)S(1)} %momentum_rows.19.mom_ref, ...), custom_call_target="tpu_custom_call" | custom-call | flops 25165824 | bytes 37748736 | tf_op jit(solution)/shard_map/cond/branch_0_fun/average_rows/pallas_call | solution.py:239
  181.4 4.3 %collective-permute-done.8.far_mom_ref = bf16[384,2048]{1,0:T(8,128)(2,1)S(1)} collective-permute-done((bf16[384,2048]{1,0:T(8,128)(2,1)S(1)}, bf16[384,2048]{1,0:T(8,128)(2,1)S(1)}, u32[]{:S(2)}, u32[]{:S(2)}) %collective-permute-start.8) | collective-permute-done | bytes 1572896 | tf_op jit(solution)/shard_map/cond/branch_0_fun/ppermute | solution.py:28
  185.7 4.3 %average_rows.9 = (bf16[1,2048,2048]{2,1,0:T(8,128)(2,1)}, bf16[1,2048,2048]{2,1,0:T(8,128)(2,1)}) custom-call(bf16[1,2048,2048]{2,1,0:T(8,128)(2,1)S(1)} %bitcast.85, bf16[1,2048,2048]{2,1,0:T(8,128)(2,1)} %collective-permute-done.far_weight_ref, bf16[384,2048]{1,0:T(8,128)(2,1)S(1)} %momentum_rows.18.mom_ref, ...), custom_call_target="tpu_custom_call", output_to_operand_aliasing={{0}: (4, {}), {1}: (5, {})} | custom-call | flops 6291456 | bytes 9437184 | tf_op jit(solution)/shard_map/cond/branch_0_fun/average_rows/pallas_call | solution.py:239
  190.1 1.4 collective-permute-done.7.refs_3_
  191.4 1.6 average_near.8
  (37 shorter events, 9.9 us)
Async XLA Ops:
  1.3 11.8 %copy-start.8 = (s32[1,128]{1,0:T(1,128)S(1)}, s32[1,128]{1,0:T(1,128)}, u32[]{:S(2)}) copy-start(s32[1,128]{1,0:T(1,128)} %get-tuple-element.66) | copy-start | bytes 1540 | tf_op jit(solution)/shard_map/cond
  2.6 15.8 %collective-permute-start.1 = (bf16[128,2048]{0,1:T(8,128)(2,1)S(1)}, bf16[128,2048]{0,1:T(8,128)(2,1)S(1)}, u32[]{:S(2)}, u32[]{:S(2)}) collective-permute-start(bf16[128,2048]{0,1:T(8,128)(2,1)S(1)} %bitcast.92), channel_id=1, source_target_pairs={{0,1},{1,0},{2,3},{3,2},{4,5},{5,4},{6,7},{7,6},{8,9},{9,8},{10,11... | collective-permute-start | bytes 1572872 | tf_op jit(solution)/shard_map/cond/branch_0_fun/ppermute | solution.py:28
  5.7 95.9 %collective-permute-start = (bf16[1,2048,2048]{2,1,0:T(8,128)(2,1)}, bf16[1,2048,2048]{2,1,0:T(8,128)(2,1)}, u32[]{:S(2)}, u32[]{:S(2)}) collective-permute-start(bf16[1,2048,2048]{2,1,0:T(8,128)(2,1)} %get-tuple-element.64.weight_ref), channel_id=1, source_target_pairs={{0,2},{2,4},{4,6},{6,8},{8,10},{10,12},{12,14},{14,16},{16,18},{18... | collective-permute-start | bytes 25165832 | tf_op jit(solution)/shard_map/cond/branch_0_fun/ppermute | solution.py:28
  8.8 32.7 %copy-start = (bf16[1,2048]{1,0:T(2,128)(2,1)S(1)}, bf16[1,2048]{1,0:T(2,128)(2,1)}, u32[]{:S(2)}) copy-start(bf16[1,2048]{1,0:T(2,128)(2,1)} %get-tuple-element.69.gain_ref) | copy-start | bytes 12292 | tf_op jit(solution)/shard_map/cond
  8.8 21.0 %collective-permute-start.3 = (bf16[128,2048]{1,0:T(8,128)(2,1)}, bf16[128,2048]{1,0:T(8,128)(2,1)}, u32[]{:S(2)}, u32[]{:S(2)}) collective-permute-start(bf16[128,2048]{1,0:T(8,128)(2,1)} %get-tuple-element.189), channel_id=1, source_target_pairs={{0,1},{1,0},{2,3},{3,2},{4,5},{5,4},{6,7},{7,6},{8,9},{9,8},{10,11... | collective-permute-start | bytes 1572872 | tf_op jit(solution)/shard_map/cond/branch_0_fun/ppermute | solution.py:28
  11.2 29.0 %collective-permute-start.2 = (bf16[128,2048]{1,0:T(8,128)(2,1)}, bf16[128,2048]{1,0:T(8,128)(2,1)}, u32[]{:S(2)}, u32[]{:S(2)}) collective-permute-start(bf16[128,2048]{1,0:T(8,128)(2,1)} %get-tuple-element.191), channel_id=1, source_target_pairs={{0,1},{1,0},{2,3},{3,2},{4,5},{5,4},{6,7},{7,6},{8,9},{9,8},{10,11... | collective-permute-start | bytes 1572872 | tf_op jit(solution)/shard_map/cond/branch_0_fun/ppermute | solution.py:28
  41.5 15.6 %copy-start.4 = (bf16[1,2048]{1,0:T(2,128)(2,1)S(1)}, bf16[1,2048]{1,0:T(2,128)(2,1)}, u32[]{:S(2)}) copy-start(bf16[1,2048]{1,0:T(2,128)(2,1)} %get-tuple-element.72.gain_momentum_ref) | copy-start | bytes 12292 | tf_op jit(solution)/shard_map/cond
  41.5 23.2 %slice-start = ((s8[8388608]{0:T(1024)(128)(4,1)}), s8[4194304]{0:T(1024)(128)(4,1)S(1)}, s32[]{:S(2)}) async-start(s8[8388608]{0:T(1024)(128)(4,1)} %bitcast.76), calls=%async_computation | async-start | bytes 8388608 | tf_op jit(solution)/shard_map/cond
  41.5 23.1 %slice-start.1 = ((s8[8388608]{0:T(1024)(128)(4,1)}), s8[4194304]{0:T(1024)(128)(4,1)S(1)}, s32[]{:S(2)}) async-start(s8[8388608]{0:T(1024)(128)(4,1)} %bitcast.76), calls=%async_computation.1 | async-start | bytes 8388608 | tf_op jit(solution)/shard_map/cond
  52.1 5.0 %collective-permute-start.4 = (f32[256,128]{1,0:T(8,128)S(1)}, f32[256,128]{1,0:T(8,128)S(1)}, u32[]{:S(2)}, u32[]{:S(2)}) collective-permute-start(f32[256,128]{1,0:T(8,128)S(1)} %get-tuple-element.71), channel_id=1, source_target_pairs={{0,1},{1,0},{2,3},{3,2},{4,5},{5,4},{6,7},{7,6},{8,9},{9,8},{10,11... | collective-permute-start | bytes 393224 | tf_op jit(solution)/shard_map/cond/branch_0_fun/ppermute | solution.py:28
  57.1 21.4 %slice-start.8 = ((s8[8388608]{0:T(1024)(128)(4,1)}), s8[4194304]{0:T(1024)(128)(4,1)S(1)}, s32[]{:S(2)}) async-start(s8[8388608]{0:T(1024)(128)(4,1)} %bitcast.84), calls=%async_computation.8 | async-start | bytes 8388608 | tf_op jit(solution)/shard_map/cond
  64.7 13.9 %slice-start.9 = ((s8[8388608]{0:T(1024)(128)(4,1)}), s8[4194304]{0:T(1024)(128)(4,1)S(1)}, s32[]{:S(2)}) async-start(s8[8388608]{0:T(1024)(128)(4,1)} %bitcast.84), calls=%async_computation.9 | async-start | bytes 8388608 | tf_op jit(solution)/shard_map/cond
  74.2 94.6 %collective-permute-start.9 = (bf16[1536,2048]{1,0:T(8,128)(2,1)S(1)}, bf16[1536,2048]{1,0:T(8,128)(2,1)S(1)}, u32[]{:S(2)}, u32[]{:S(2)}) collective-permute-start(bf16[1536,2048]{1,0:T(8,128)(2,1)S(1)} %momentum_rows.19.mom_ref), channel_id=1, source_target_pairs={{0,2},{2,4},{4,6},{6,8},{8,10},{10,12},{12,14},{14,16},{16,18},{18... | collective-permute-start | bytes 18874376 | tf_op jit(solution)/shard_map/cond/branch_0_fun/ppermute | solution.py:28
  76.7 109.0 %collective-permute-start.8 = (bf16[384,2048]{1,0:T(8,128)(2,1)S(1)}, bf16[384,2048]{1,0:T(8,128)(2,1)S(1)}, u32[]{:S(2)}, u32[]{:S(2)}) collective-permute-start(bf16[384,2048]{1,0:T(8,128)(2,1)S(1)} %momentum_rows.18.mom_ref), channel_id=1, source_target_pairs={{0,2},{2,4},{4,6},{6,8},{8,10},{10,12},{12,14},{14,16},{16,18},{18... | collective-permute-start | bytes 4718600 | tf_op jit(solution)/shard_map/cond/branch_0_fun/ppermute | solution.py:28
  78.6 114.5 %collective-permute-start.6 = (bf16[2,2048]{1,0:T(2,128)(2,1)S(1)}, bf16[2,2048]{1,0:T(2,128)(2,1)S(1)}, u32[]{:S(2)}, u32[]{:S(2)}) collective-permute-start(bf16[2,2048]{1,0:T(2,128)(2,1)S(1)} %get-tuple-element.75.refs_4_), channel_id=1, source_target_pairs={{0,2},{2,4},{4,6},{6,8},{8,10},{10,12},{12,14},{14,16},{16,18},{18... | collective-permute-start | bytes 24584 | tf_op jit(solution)/shard_map/cond/branch_0_fun/ppermute | solution.py:28
  79.3 113.7 %collective-permute-start.5 = (bf16[32,2048]{1,0:T(8,128)(2,1)S(1)}, bf16[32,2048]{1,0:T(8,128)(2,1)S(1)}, u32[]{:S(2)}, u32[]{:S(2)}) collective-permute-start(bf16[32,2048]{1,0:T(8,128)(2,1)S(1)} %momentum_rows.16.refs_2_), channel_id=1, source_target_pairs={{0,2},{2,4},{4,6},{6,8},{8,10},{10,12},{12,14},{14,16},{16,18},{18... | collective-permute-start | bytes 393224 | tf_op jit(solution)/shard_map/cond/branch_0_fun/ppermute | solution.py:28
  101.6 89.9 %collective-permute-start.7 = (bf16[96,2048]{1,0:T(8,128)(2,1)S(1)}, bf16[96,2048]{1,0:T(8,128)(2,1)S(1)}, u32[]{:S(2)}, u32[]{:S(2)}) collective-permute-start(bf16[96,2048]{1,0:T(8,128)(2,1)S(1)} %momentum_rows.17.refs_2_), channel_id=1, source_target_pairs={{0,2},{2,4},{4,6},{6,8},{8,10},{10,12},{12,14},{14,16},{16,18},{18... | collective-permute-start | bytes 1179656 | tf_op jit(solution)/shard_map/cond/branch_0_fun/ppermute | solution.py:28
where the time goes:
time: 195 us; the launch traced here: 194 us
  waiting for transfers between devices  118 us (61%)
  Pallas kernels  51.7 us (27%)
  starting transfers between devices  10.5 us (5%)
  local copies, waits for them, and re-layouts  6.46 us (3%)
  other arithmetic  5.38 us (3%)
    ppermute x10, waiting for transfers between devices, passed_along(): lax.ppermute(array, axis, [(i, (i + by) % peers) for i in range(peers)])  118 us
    pallas_call x2, Pallas kernels, average_rows(): pl.pallas_call(average_rows_kernel, grid=(rows // block,), in_specs=[whol...  16.9 us
    pallas_call x4, Pallas kernels, momentum_rows(): pl.pallas_call(momentum_rows_kernel, grid=(rows // block,), in_specs=[pl....  14.4 us
    ppermute x10, starting transfers between devices, passed_along(): lax.ppermute(array, axis, [(i, (i + by) % peers) for i in range(peers)])  10.5 us
    pallas_call x1, Pallas kernels, forward(): pl.pallas_call(forward_kernel, grid=(columns // block,), in_specs=[pl.Blo...  10.5 us
    pallas_call x1, Pallas kernels, gradient(): pl.pallas_call(functools.partial(gradient_kernel, width), grid=(columns /...  7.52 us
  transfers between devices with their start and end apart: 10, of which 8 were waited for; matrix products, arithmetic and copies ran while one was open for 5% of the time, Pallas kernels for 26%

commit v1 on v0

--- a/solution.py
+++ b/solution.py
@@ -17,7 +17,7 @@
 LEARN_RATE = 0.05
 
 
-SHARES = (48, 12, 3, 1)
+SHARES = (24, 6, 1, 1)
 NEAR = 2
 LANES = 128
 TILE = 16
@@ -267,7 +267,7 @@
 
 def average_near(weight, far_weight, mom, far_mom, held, first, weight_first, gains):
     rows, columns = mom.shape
-    block = math.gcd(first, rows, 32)
+    block = math.gcd(first, rows, 16)
     skip = first // block
     inputs = (weight, far_weight, mom, far_mom, *gains)
     whole = pl.BlockSpec((None, block, columns), lambda i: (0, skip + i, 0))
@@ -297,11 +297,12 @@
     norm_gain,
     momentum,
     gain_momentum,
+    me,
     *,
     level,
 ):
     distance = 1 << level
-    me, peers = lax.axis_index("fsdp"), lax.axis_size("fsdp")
+    peers = lax.axis_size("fsdp")
     tokens = contexts.shape[1]
     hidden, columns = weight.shape[1:]
 
@@ -365,7 +366,7 @@
 
     branches = [branch(level) for level in range(levels)]
     return lax.switch(
-        lax.rem(step_index[0], levels),
+        step_index[0] % levels,
         branches,
         contexts,
         residual,
@@ -375,6 +376,7 @@
         norm_gain,
         momentum,
         gain_momentum,
+        lax.axis_index("fsdp"),
     )
 
 

time: 195 us -> 195 us (level)
  transfers between devices with their start and end apart: 10 -> 10, of which waited for: 8 -> 8; matrix products, arithmetic and copies ran while one was open for 5% -> 5% of each run, Pallas kernels for 26% -> 25%
where the time goes in v1:
time: 195 us
  waiting for transfers between devices  119 us (61%)
  Pallas kernels  51.1 us (26%)
  starting transfers between devices  10.6 us (5%)
  local copies, waits for them, and re-layouts  6.46 us (3%)
  other arithmetic  5.38 us (3%)
    ppermute x10, waiting for transfers between devices, passed_along(): lax.ppermute(array, axis, [(i, (i + by) % peers) for i in range(peers)])  119 us
    pallas_call x2, Pallas kernels, average_rows(): pl.pallas_call(average_rows_kernel, grid=(rows // block,), in_specs=[whol...  16.9 us
    pallas_call x4, Pallas kernels, momentum_rows(): pl.pallas_call(momentum_rows_kernel, grid=(rows // block,), in_specs=[pl....  13.2 us
    ppermute x10, starting transfers between devices, passed_along(): lax.ppermute(array, axis, [(i, (i + by) % peers) for i in range(peers)])  10.6 us
    pallas_call x1, Pallas kernels, forward(): pl.pallas_call(forward_kernel, grid=(columns // block,), in_specs=[pl.Blo...  10.5 us
    pallas_call x1, Pallas kernels, gradient(): pl.pallas_call(functools.partial(gradient_kernel, width), grid=(columns /...  7.52 us
  transfers between devices with their start and end apart: 10, of which 8 were waited for; matrix products, arithmetic and copies ran while one was open for 5% of the time, Pallas kernels for 25%

profile of v1, /device:TPU:0, one launch (start us, length us, event | category | flops | bytes accessed | tf_op | source)
XLA Modules:
  0.0 194.7 jit_solution(1986224836525773587)
XLA Ops:
  1.3 193.2 %conditional.1 = (bf16[1,2048,2048]{2,1,0:T(8,128)(2,1)}, bf16[1,2048]{1,0:T(2,128)(2,1)}, bf16[1,2048,2048]{2,1,0:T(8,128)(2,1)}, bf16[1,2048]{1,0:T(2,128)(2,1)}) conditional(s32[]{:T(128)} %clamp.3, (bf16[1,2048,2048]{2,1,0:T(8,128)(2,1)}, bf16[1,128,2048]{2,1,0:T(8,128)(2,1)}, s32[1,128]{1,0:T(1,128)}, s32[]{:T(128)}, ...), branch_computations={%region_0.2_spmd, %region_2.4_spmd, %region_4.6_spmd, %region_6.8_... | conditional | flops 4341694976 | bytes 234303552 | solution.py:368
  2.6 3.1 %collective-permute-start.1 = (bf16[128,2048]{0,1:T(8,128)(2,1)S(1)}, bf16[128,2048]{0,1:T(8,128)(2,1)S(1)}, u32[]{:S(2)}, u32[]{:S(2)}) collective-permute-start(bf16[128,2048]{0,1:T(8,128)(2,1)S(1)} %bitcast.92), channel_id=1, source_target_pairs={{0,1},{1,0},{2,3},{3,2},{4,5},{5,4},{6,7},{7,6},{8,9},{9,8},{10,11... | collective-permute-start | bytes 1572872 | tf_op jit(solution)/shard_map/cond/branch_0_fun/ppermute | solution.py:28
  6.4 1.4 bitcast_select_fusion
  8.9 2.3 %dynamic-slice_bitcast_fusion.1 = (bf16[128,2048]{1,0:T(8,128)(2,1)}, bf16[128,2048]{1,0:T(8,128)(2,1)}) fusion(bf16[1,128,4096]{2,1,0:T(8,128)(2,1)} %get-tuple-element.75, s32[]{:T(128)S(6)} %select_n.59, s32[]{:T(128)S(6)} %select_n.61), kind=kLoop, calls=%fused_computation.6 | loop fusion | bytes 2097160 | tf_op jit(solution)/shard_map/cond/branch_0_fun/dynamic_slice | solution.py:318
  11.2 1.9 collective-permute-start.2
  13.7 4.8 %collective-permute-done.1 = bf16[128,2048]{0,1:T(8,128)(2,1)S(1)} collective-permute-done((bf16[128,2048]{0,1:T(8,128)(2,1)S(1)}, bf16[128,2048]{0,1:T(8,128)(2,1)S(1)}, u32[]{:S(2)}, u32[]{:S(2)}) %collective-permute-start.1) | collective-permute-done | bytes 524320 | tf_op jit(solution)/shard_map/cond/branch_0_fun/ppermute | solution.py:28
  19.3 10.5 %collective-permute-done.3 = bf16[128,2048]{1,0:T(8,128)(2,1)} collective-permute-done((bf16[128,2048]{1,0:T(8,128)(2,1)}, bf16[128,2048]{1,0:T(8,128)(2,1)}, u32[]{:S(2)}, u32[]{:S(2)}) %collective-permute-start.3) | collective-permute-done | bytes 524320 | tf_op jit(solution)/shard_map/cond/branch_0_fun/ppermute | solution.py:28
  31.1 9.1 %collective-permute-done.2 = bf16[128,2048]{1,0:T(8,128)(2,1)} collective-permute-done((bf16[128,2048]{1,0:T(8,128)(2,1)}, bf16[128,2048]{1,0:T(8,128)(2,1)}, u32[]{:S(2)}, u32[]{:S(2)}) %collective-permute-start.2) | collective-permute-done | bytes 524320 | tf_op jit(solution)/shard_map/cond/branch_0_fun/ppermute | solution.py:28
  41.6 10.5 %forward.4 = (f32[256,2048]{1,0:T(8,128)S(1)}, f32[256,128]{1,0:T(8,128)S(1)}) custom-call(f32[1]{0:T(128)} %bitcast.5.count_ref, bf16[256,2048]{1,0:T(8,128)(2,1)S(1)} %copy.37.ctx_ref, bf16[1,2048,2048]{2,1,0:T(8,128)(2,1)} %get-tuple-element.72.weight_ref, bf16[256,2048]{1,0:T(8,128)(2,1)S(1)} %pad_maximum_fusion.1.resid_ref, ...), custom_call_target="tpu_custom_call" | custom-call | flops 2147483648 | bytes 13762560 | tf_op jit(solution)/shard_map/cond/branch_0_fun/forward/pallas_call | solution.py:81
  52.1 1.8 collective-permute-start.4
  53.9 3.2 %collective-permute-done.4 = f32[256,128]{1,0:T(8,128)S(1)} collective-permute-done((f32[256,128]{1,0:T(8,128)S(1)}, f32[256,128]{1,0:T(8,128)S(1)}, u32[]{:S(2)}, u32[]{:S(2)}) %collective-permute-start.4) | collective-permute-done | bytes 131104 | tf_op jit(solution)/shard_map/cond/branch_0_fun/ppermute | solution.py:28
  57.2 7.5 %gradient.4 = (bf16[256,2048]{1,0:T(8,128)(2,1)S(1)}, bf16[2,2048]{1,0:T(2,128)(2,1)S(1)}) custom-call(f32[256,2048]{1,0:T(8,128)S(1)} %get-tuple-element.79.pre_ref, bf16[256,2048]{1,0:T(8,128)(2,1)S(1)} %pad_maximum_fusion.2.cotan_ref, f32[256,128]{1,0:T(8,128)S(1)} %maximum_add_fusion.sums_ref, bf16[1,2048]{1,0:T(2,128)(2,1)S(1)} %copy-done, ...), custom_call_target="tpu_custom_call" | custom-call | flops 6291456 | bytes 4333568 | tf_op jit(solution)/shard_map/cond/branch_0_fun/gradient/pallas_call | solution.py:140
  64.7 9.5 %momentum_rows.19.mom_ref = bf16[1536,2048]{1,0:T(8,128)(2,1)S(1)} custom-call(bf16[2048,256]{1,0:T(8,128)(2,1)S(1)} %get-tuple-element.209.ctx_ref, bf16[256,2048]{1,0:T(8,128)(2,1)S(1)} %get-tuple-element.82.grad_ref, bf16[1,2048,2048]{2,1,0:T(8,128)(2,1)S(1)} %bitcast.77), custom_call_target="tpu_custom_call" | custom-call | flops 1610612736 | bytes 14417920 | tf_op jit(solution)/shard_map/cond/branch_0_fun/momentum_rows/pallas_call | solution.py:175
  74.3 2.4 %momentum_rows.18.mom_ref = bf16[384,2048]{1,0:T(8,128)(2,1)S(1)} custom-call(bf16[2048,256]{1,0:T(8,128)(2,1)S(1)} %get-tuple-element.209.ctx_ref, bf16[256,2048]{1,0:T(8,128)(2,1)S(1)} %get-tuple-element.82.grad_ref, bf16[1,2048,2048]{2,1,0:T(8,128)(2,1)S(1)} %bitcast.77), custom_call_target="tpu_custom_call" | custom-call | flops 402653184 | bytes 4390912 | tf_op jit(solution)/shard_map/cond/branch_0_fun/momentum_rows/pallas_call | solution.py:175
  76.7 1.8 collective-permute-start.8
  79.4 1.7 collective-permute-start.5
  81.7 19.9 %collective-permute-done.far_weight_ref = bf16[1,2048,2048]{2,1,0:T(8,128)(2,1)} collective-permute-done((bf16[1,2048,2048]{2,1,0:T(8,128)(2,1)}, bf16[1,2048,2048]{2,1,0:T(8,128)(2,1)}, u32[]{:S(2)}, u32[]{:S(2)}) %collective-permute-start) | collective-permute-done | bytes 8388640 | tf_op jit(solution)/shard_map/cond/branch_0_fun/ppermute | solution.py:28
  102.7 66.2 %collective-permute-done.9.far_mom_ref = bf16[1536,2048]{1,0:T(8,128)(2,1)S(1)} collective-permute-done((bf16[1536,2048]{1,0:T(8,128)(2,1)S(1)}, bf16[1536,2048]{1,0:T(8,128)(2,1)S(1)}, u32[]{:S(2)}, u32[]{:S(2)}) %collective-permute-start.9) | collective-permute-done | bytes 6291488 | tf_op jit(solution)/shard_map/cond/branch_0_fun/ppermute | solution.py:28
  168.9 12.5 %average_rows.8 = (bf16[1,2048,2048]{2,1,0:T(8,128)(2,1)}, bf16[1,2048,2048]{2,1,0:T(8,128)(2,1)}) custom-call(bf16[1,2048,2048]{2,1,0:T(8,128)(2,1)S(1)} %bitcast.85, bf16[1,2048,2048]{2,1,0:T(8,128)(2,1)} %collective-permute-done.far_weight_ref, bf16[1536,2048]{1,0:T(8,128)(2,1)S(1)} %momentum_rows.19.mom_ref, ...), custom_call_target="tpu_custom_call" | custom-call | flops 25165824 | bytes 37748736 | tf_op jit(solution)/shard_map/cond/branch_0_fun/average_rows/pallas_call | solution.py:239
  181.4 4.3 %collective-permute-done.8.far_mom_ref = bf16[384,2048]{1,0:T(8,128)(2,1)S(1)} collective-permute-done((bf16[384,2048]{1,0:T(8,128)(2,1)S(1)}, bf16[384,2048]{1,0:T(8,128)(2,1)S(1)}, u32[]{:S(2)}, u32[]{:S(2)}) %collective-permute-start.8) | collective-permute-done | bytes 1572896 | tf_op jit(solution)/shard_map/cond/branch_0_fun/ppermute | solution.py:28
  185.8 4.3 %average_rows.9 = (bf16[1,2048,2048]{2,1,0:T(8,128)(2,1)}, bf16[1,2048,2048]{2,1,0:T(8,128)(2,1)}) custom-call(bf16[1,2048,2048]{2,1,0:T(8,128)(2,1)S(1)} %bitcast.85, bf16[1,2048,2048]{2,1,0:T(8,128)(2,1)} %collective-permute-done.far_weight_ref, bf16[384,2048]{1,0:T(8,128)(2,1)S(1)} %momentum_rows.18.mom_ref, ...), custom_call_target="tpu_custom_call", output_to_operand_aliasing={{0}: (4, {}), {1}: (5, {})} | custom-call | flops 6291456 | bytes 9437184 | tf_op jit(solution)/shard_map/cond/branch_0_fun/average_rows/pallas_call | solution.py:239
  190.1 1.4 collective-permute-done.7.refs_3_
  191.5 1.5 average_near.8
  192.9 1.5 average_near.9
  (37 shorter events, 9.8 us)
Async XLA Ops:
  1.3 11.8 %copy-start.8 = (s32[1,128]{1,0:T(1,128)S(1)}, s32[1,128]{1,0:T(1,128)}, u32[]{:S(2)}) copy-start(s32[1,128]{1,0:T(1,128)} %get-tuple-element.74) | copy-start | bytes 1540 | tf_op jit(solution)/shard_map/cond
  2.6 15.8 %collective-permute-start.1 = (bf16[128,2048]{0,1:T(8,128)(2,1)S(1)}, bf16[128,2048]{0,1:T(8,128)(2,1)S(1)}, u32[]{:S(2)}, u32[]{:S(2)}) collective-permute-start(bf16[128,2048]{0,1:T(8,128)(2,1)S(1)} %bitcast.92), channel_id=1, source_target_pairs={{0,1},{1,0},{2,3},{3,2},{4,5},{5,4},{6,7},{7,6},{8,9},{9,8},{10,11... | collective-permute-start | bytes 1572872 | tf_op jit(solution)/shard_map/cond/branch_0_fun/ppermute | solution.py:28
  5.7 95.9 %collective-permute-start = (bf16[1,2048,2048]{2,1,0:T(8,128)(2,1)}, bf16[1,2048,2048]{2,1,0:T(8,128)(2,1)}, u32[]{:S(2)}, u32[]{:S(2)}) collective-permute-start(bf16[1,2048,2048]{2,1,0:T(8,128)(2,1)} %get-tuple-element.72.weight_ref), channel_id=1, source_target_pairs={{0,2},{2,4},{4,6},{6,8},{8,10},{10,12},{12,14},{14,16},{16,18},{18... | collective-permute-start | bytes 25165832 | tf_op jit(solution)/shard_map/cond/branch_0_fun/ppermute | solution.py:28
  8.8 32.7 %copy-start = (bf16[1,2048]{1,0:T(2,128)(2,1)S(1)}, bf16[1,2048]{1,0:T(2,128)(2,1)}, u32[]{:S(2)}) copy-start(bf16[1,2048]{1,0:T(2,128)(2,1)} %get-tuple-element.78.gain_ref) | copy-start | bytes 12292 | tf_op jit(solution)/shard_map/cond
  8.8 21.0 %collective-permute-start.3 = (bf16[128,2048]{1,0:T(8,128)(2,1)}, bf16[128,2048]{1,0:T(8,128)(2,1)}, u32[]{:S(2)}, u32[]{:S(2)}) collective-permute-start(bf16[128,2048]{1,0:T(8,128)(2,1)} %get-tuple-element.205), channel_id=1, source_target_pairs={{0,1},{1,0},{2,3},{3,2},{4,5},{5,4},{6,7},{7,6},{8,9},{9,8},{10,11... | collective-permute-start | bytes 1572872 | tf_op jit(solution)/shard_map/cond/branch_0_fun/ppermute | solution.py:28
  11.2 29.0 %collective-permute-start.2 = (bf16[128,2048]{1,0:T(8,128)(2,1)}, bf16[128,2048]{1,0:T(8,128)(2,1)}, u32[]{:S(2)}, u32[]{:S(2)}) collective-permute-start(bf16[128,2048]{1,0:T(8,128)(2,1)} %get-tuple-element.207), channel_id=1, source_target_pairs={{0,1},{1,0},{2,3},{3,2},{4,5},{5,4},{6,7},{7,6},{8,9},{9,8},{10,11... | collective-permute-start | bytes 1572872 | tf_op jit(solution)/shard_map/cond/branch_0_fun/ppermute | solution.py:28
  41.5 15.6 %copy-start.4 = (bf16[1,2048]{1,0:T(2,128)(2,1)S(1)}, bf16[1,2048]{1,0:T(2,128)(2,1)}, u32[]{:S(2)}) copy-start(bf16[1,2048]{1,0:T(2,128)(2,1)} %get-tuple-element.81.gain_momentum_ref) | copy-start | bytes 12292 | tf_op jit(solution)/shard_map/cond
  41.5 23.2 %slice-start = ((s8[8388608]{0:T(1024)(128)(4,1)}), s8[4194304]{0:T(1024)(128)(4,1)S(1)}, s32[]{:S(2)}) async-start(s8[8388608]{0:T(1024)(128)(4,1)} %bitcast.76), calls=%async_computation | async-start | bytes 8388608 | tf_op jit(solution)/shard_map/cond
  41.5 23.1 %slice-start.1 = ((s8[8388608]{0:T(1024)(128)(4,1)}), s8[4194304]{0:T(1024)(128)(4,1)S(1)}, s32[]{:S(2)}) async-start(s8[8388608]{0:T(1024)(128)(4,1)} %bitcast.76), calls=%async_computation.1 | async-start | bytes 8388608 | tf_op jit(solution)/shard_map/cond
  52.1 5.0 %collective-permute-start.4 = (f32[256,128]{1,0:T(8,128)S(1)}, f32[256,128]{1,0:T(8,128)S(1)}, u32[]{:S(2)}, u32[]{:S(2)}) collective-permute-start(f32[256,128]{1,0:T(8,128)S(1)} %get-tuple-element.80), channel_id=1, source_target_pairs={{0,1},{1,0},{2,3},{3,2},{4,5},{5,4},{6,7},{7,6},{8,9},{9,8},{10,11... | collective-permute-start | bytes 393224 | tf_op jit(solution)/shard_map/cond/branch_0_fun/ppermute | solution.py:28
  57.1 21.4 %slice-start.8 = ((s8[8388608]{0:T(1024)(128)(4,1)}), s8[4194304]{0:T(1024)(128)(4,1)S(1)}, s32[]{:S(2)}) async-start(s8[8388608]{0:T(1024)(128)(4,1)} %bitcast.84), calls=%async_computation.8 | async-start | bytes 8388608 | tf_op jit(solution)/shard_map/cond
  64.7 13.9 %slice-start.9 = ((s8[8388608]{0:T(1024)(128)(4,1)}), s8[4194304]{0:T(1024)(128)(4,1)S(1)}, s32[]{:S(2)}) async-start(s8[8388608]{0:T(1024)(128)(4,1)} %bitcast.84), calls=%async_computation.9 | async-start | bytes 8388608 | tf_op jit(solution)/shard_map/cond
  74.3 94.6 %collective-permute-start.9 = (bf16[1536,2048]{1,0:T(8,128)(2,1)S(1)}, bf16[1536,2048]{1,0:T(8,128)(2,1)S(1)}, u32[]{:S(2)}, u32[]{:S(2)}) collective-permute-start(bf16[1536,2048]{1,0:T(8,128)(2,1)S(1)} %momentum_rows.19.mom_ref), channel_id=1, source_target_pairs={{0,2},{2,4},{4,6},{6,8},{8,10},{10,12},{12,14},{14,16},{16,18},{18... | collective-permute-start | bytes 18874376 | tf_op jit(solution)/shard_map/cond/branch_0_fun/ppermute | solution.py:28
  76.7 109.0 %collective-permute-start.8 = (bf16[384,2048]{1,0:T(8,128)(2,1)S(1)}, bf16[384,2048]{1,0:T(8,128)(2,1)S(1)}, u32[]{:S(2)}, u32[]{:S(2)}) collective-permute-start(bf16[384,2048]{1,0:T(8,128)(2,1)S(1)} %momentum_rows.18.mom_ref), channel_id=1, source_target_pairs={{0,2},{2,4},{4,6},{6,8},{8,10},{10,12},{12,14},{14,16},{16,18},{18... | collective-permute-start | bytes 4718600 | tf_op jit(solution)/shard_map/cond/branch_0_fun/ppermute | solution.py:28
  78.6 114.3 %collective-permute-start.6 = (bf16[2,2048]{1,0:T(2,128)(2,1)S(1)}, bf16[2,2048]{1,0:T(2,128)(2,1)S(1)}, u32[]{:S(2)}, u32[]{:S(2)}) collective-permute-start(bf16[2,2048]{1,0:T(2,128)(2,1)S(1)} %get-tuple-element.84.refs_4_), channel_id=1, source_target_pairs={{0,2},{2,4},{4,6},{6,8},{8,10},{10,12},{12,14},{14,16},{16,18},{18... | collective-permute-start | bytes 24584 | tf_op jit(solution)/shard_map/cond/branch_0_fun/ppermute | solution.py:28
  79.4 113.6 %collective-permute-start.5 = (bf16[64,2048]{1,0:T(8,128)(2,1)S(1)}, bf16[64,2048]{1,0:T(8,128)(2,1)S(1)}, u32[]{:S(2)}, u32[]{:S(2)}) collective-permute-start(bf16[64,2048]{1,0:T(8,128)(2,1)S(1)} %momentum_rows.16.refs_2_), channel_id=1, source_target_pairs={{0,2},{2,4},{4,6},{6,8},{8,10},{10,12},{12,14},{14,16},{16,18},{18... | collective-permute-start | bytes 786440 | tf_op jit(solution)/shard_map/cond/branch_0_fun/ppermute | solution.py:28
  101.6 89.9 %collective-permute-start.7 = (bf16[64,2048]{1,0:T(8,128)(2,1)S(1)}, bf16[64,2048]{1,0:T(8,128)(2,1)S(1)}, u32[]{:S(2)}, u32[]{:S(2)}) collective-permute-start(bf16[64,2048]{1,0:T(8,128)(2,1)S(1)} %momentum_rows.17.refs_2_), channel_id=1, source_target_pairs={{0,2},{2,4},{4,6},{6,8},{8,10},{10,12},{12,14},{14,16},{16,18},{18... | collective-permute-start | bytes 786440 | tf_op jit(solution)/shard_map/cond/branch_0_fun/ppermute | solution.py:28
